TPU v7x, 512 devices: a whole 4x8x8 slice. The times are simulated.
512 devices in a mesh: section: 16 (over x, y_lo, core), tensor: 32 (over y_hi, z).
Axes of the slice: x: 4, y: 8 (y_hi: 4, y_lo: 2; y = y_hi * 2 + y_lo), z: 8, core: 2. Of those that a mesh axis runs over, the one named last changes fastest.
Arguments:
- hidden: bfloat16 [16, 256, 8192], P('section', 'tensor'), may hold values from -60 to 60
- norm_gain: float32 [8192], replicated, may hold values from 0.1 to 1.9
- lengths: int32 [16], P('section'), may hold values from 64 to 256
- query_param: float32 [8192, 4096], P(('section', 'tensor')), may hold values from -1.3258252 to 1.3258252
- query_grad: float32 [8192, 4096], P(('section', 'tensor')), may hold values from -0.006 to 0.006
- query_moment: float32 [8192, 4096], P(('section', 'tensor')), may hold values from -0.006 to 0.006
- query_second: float32 [8192, 4096], P(('section', 'tensor')), may hold values from 1e-07 to 1e-05
- keyval_param: float32 [8192, 1024], P(('section', 'tensor')), may hold values from -0.06629126 to 0.06629126
- keyval_gradient: float32 [8192, 1024], P(('section', 'tensor')), may hold values from -0.006 to 0.006
- keyval_first_moment: float32 [8192, 1024], P(('section', 'tensor')), may hold values from -0.006 to 0.006
- keyval_second_moment: float32 [8192, 1024], P(('section', 'tensor')), may hold values from 1e-07 to 1e-05
- output_param: float32 [8192, 4096], P(('section', 'tensor')), may hold values from -0.25 to 0.25
- output_grad: float32 [8192, 4096], P(('section', 'tensor')), may hold values from -0.006 to 0.006
- output_moment: float32 [8192, 4096], P(('section', 'tensor')), may hold values from -0.006 to 0.006
- output_second: float32 [8192, 4096], P(('section', 'tensor')), may hold values from 1e-07 to 1e-05
Outputs:
- mixed: bfloat16 [16, 256, 8192], P('section', 'tensor')
All inputs are finite; a program needn't handle non-finite values.
Results may differ from a plain program's by a relative error of at most 0.017.
Values may be sent and summed in bfloat16 or wider, within the bound.
No kernel may reach another device: no remote copies, remote signals or barrier semaphores. Data moves between devices by JAX's collectives and lax.ppermute only.
A program may use at most 64 MiB of HBM per device.

v0:
```python
import math
import jax
import jax.numpy as jnp
from jax import lax
from jax.sharding import PartitionSpec as P

QUERY_HEADS_LOCAL = 32
KEYVAL_HEADS = 4
HEAD_DIMENSION = 128
learn_rate = 0.015
beta_one = 0.5
beta_two = 0.9
adam_step = 1000.0
adam_eps = 1e-08
decay_rate = 0.1
norm_eps = 1e-06
rope_base = 1000000.0
masked_score = -1e30


def adam_update(current, gradient, moment, second):
    moment_new = beta_one * moment + (1.0 - beta_one) * gradient
    second_new = beta_two * second + (1.0 - beta_two) * gradient * gradient
    corrected = moment_new / (1.0 - beta_one**adam_step)
    denominator = jnp.sqrt(second_new / (1.0 - beta_two**adam_step)) + adam_eps
    return (current - learn_rate * (corrected / denominator + decay_rate * current)).astype(
        jnp.bfloat16
    )


def normalize(hidden, norm_gain):
    values = hidden.astype(jnp.float32)
    factor = lax.rsqrt(jnp.mean(values * values, axis=-1, keepdims=True) + norm_eps)
    return (values * factor * norm_gain).astype(jnp.bfloat16)


def rotary_embed(values, token_positions):
    half_width = values.shape[-1] // 2
    frequency = rope_base ** (-jnp.arange(half_width, dtype=jnp.float32) * 2.0 / values.shape[-1])
    angles = token_positions.astype(jnp.float32)[:, None] * frequency[None, :]
    cosine_table = jnp.concatenate([jnp.cos(angles), jnp.cos(angles)], axis=-1)
    sine_table = jnp.concatenate([jnp.sin(angles), jnp.sin(angles)], axis=-1)
    first_half = values[..., :half_width]
    second_half = values[..., half_width:]
    rotated = jnp.concatenate([-second_half, first_half], axis=-1)
    return values * cosine_table + rotated * sine_table


def on_device(
    hidden,
    norm_gain,
    lengths,
    query_param,
    query_grad,
    query_moment,
    query_second,
    keyval_param,
    keyval_gradient,
    keyval_first_moment,
    keyval_second_moment,
    output_param,
    output_grad,
    output_moment,
    output_second,
):
    tensor_count = lax.axis_size("tensor")
    query_weight = adam_update(query_param, query_grad, query_moment, query_second)
    keyval_matrix = adam_update(
        keyval_param, keyval_gradient, keyval_first_moment, keyval_second_moment
    )
    output_weight = adam_update(output_param, output_grad, output_moment, output_second)
    local_rows = normalize(hidden[0], norm_gain)
    normed = lax.all_gather(local_rows, "tensor", axis=0, tiled=True)
    sequence = normed.shape[0]
    model_width = normed.shape[1]
    weight_row_block = query_weight.shape[0]
    heads_here = QUERY_HEADS_LOCAL // tensor_count
    head_columns = heads_here * HEAD_DIMENSION
    head_copies = tensor_count // KEYVAL_HEADS
    spread_heads = keyval_matrix.reshape(weight_row_block, 2, KEYVAL_HEADS, HEAD_DIMENSION)
    spread_heads = (
        jnp.repeat(spread_heads, head_copies, axis=2)
        .transpose(0, 2, 1, 3)
        .reshape(weight_row_block, tensor_count * 2 * HEAD_DIMENSION)
    )
    keyval_columns = spread_heads.shape[1] // tensor_count
    query_start = jnp.zeros((sequence, head_columns), jnp.float32)
    keyval_start = jnp.zeros((sequence, keyval_columns), jnp.float32)
    query_slice, keyval_slice, output_slice = (
        lax.all_to_all(query_weight, "tensor", split_axis=1, concat_axis=0, tiled=True),
        lax.all_to_all(spread_heads, "tensor", split_axis=1, concat_axis=0, tiled=True),
        lax.all_to_all(output_weight, "tensor", split_axis=1, concat_axis=0, tiled=True),
    )
    initial = (query_start, keyval_start, jnp.zeros((model_width, head_columns), jnp.bfloat16))
    offset = jnp.int32(0)
    query_total = initial[0]
    query_rows = lax.all_gather(query_slice, "section", axis=0, tiled=True)
    keyval_rows = lax.all_gather(keyval_slice, "section", axis=0, tiled=True)
    columns = lax.dynamic_slice_in_dim(normed, offset, query_rows.shape[0], 1)
    query_total = query_total + jnp.dot(columns, query_rows, preferred_element_type=jnp.float32)
    keyval_total = jnp.dot(columns, keyval_rows, preferred_element_type=jnp.float32)
    query_total, keyval_total = (query_total, keyval_total)
    out_buffer = lax.dynamic_update_slice_in_dim(
        initial[2], lax.all_gather(output_slice, "section", axis=0, tiled=True), offset, 0
    )
    key_block = keyval_total[:, :HEAD_DIMENSION]
    value_block = keyval_total[:, HEAD_DIMENSION:]
    token_positions = jnp.arange(sequence)
    query_heads = rotary_embed(
        query_total.reshape(sequence, heads_here, HEAD_DIMENSION).transpose(1, 0, 2),
        token_positions,
    ).astype(jnp.bfloat16)
    key_head_rows = rotary_embed(key_block, token_positions).astype(jnp.bfloat16)
    value_head_rows = value_block.astype(jnp.bfloat16)
    scores = jnp.einsum(
        "hqd,kd->hqk", query_heads, key_head_rows, preferred_element_type=jnp.float32
    ) / math.sqrt(HEAD_DIMENSION)
    allowed = (token_positions[None, :] <= token_positions[:, None]) & (
        token_positions[None, :] < lengths[0]
    )
    scores = jnp.where(allowed[None], scores, masked_score)
    row_max = jnp.max(scores, axis=-1, keepdims=True)
    exponent = jnp.exp(scores - row_max)
    attention = (exponent / jnp.sum(exponent, axis=-1, keepdims=True)).astype(jnp.bfloat16)
    head_out = jnp.einsum(
        "hqk,kd->hqd", attention, value_head_rows, preferred_element_type=jnp.float32
    ).astype(jnp.bfloat16)
    head_out = head_out.transpose(1, 0, 2).reshape(sequence, head_columns)
    mixed = lax.psum_scatter(
        lax.dot_general(
            head_out, out_buffer, (((1,), (1,)), ((), ())), preferred_element_type=jnp.float32
        ).astype(jnp.bfloat16),
        "tensor",
        scatter_dimension=0,
        tiled=True,
    )
    return mixed[None]


def solution(mesh):
    return jax.shard_map(
        on_device,
        mesh=mesh,
        in_specs=(
            P("section", "tensor", None),
            P(),
            P("section"),
            P(("section", "tensor"), None),
            P(("section", "tensor"), None),
            P(("section", "tensor"), None),
            P(("section", "tensor"), None),
            P(("section", "tensor"), None),
            P(("section", "tensor"), None),
            P(("section", "tensor"), None),
            P(("section", "tensor"), None),
            P(("section", "tensor"), None),
            P(("section", "tensor"), None),
            P(("section", "tensor"), None),
            P(("section", "tensor"), None),
        ),
        out_specs=P("section", "tensor", None),
        check_vma=False,
    )
```

profile of v0, /device:TPU:2, one launch (start us, length us, event | category | flops | bytes accessed | tf_op | source)
XLA Modules:
  0.0 503.8 jit_solution(8124403716524646474)
XLA Ops:
  6.5 0.0 copy-start
  6.5 0.0 copy-start.1
  6.5 0.0 copy-start.3
  6.5 0.0 copy-start.2
  6.5 0.0 all-gather.7.cloned.1.call-start
  6.6 1.5 copy_bitcast_fusion.1
  8.0 28.5 %all_to_all.57 = bf16[16,32,128]{2,0,1:T(8,128)(2,1)} all-to-all(bf16[16,32,128]{2,0,1:T(8,128)(2,1)S(1)} %copy_bitcast_fusion.1), channel_id=1, replica_groups=mesh['section'=16,'tensor'=32] {'tensor'}, dimensions={1} | all-to-all | bytes 262144 | tf_op jit(solution)/shard_map/all_to_all | solution.py:90
  36.5 0.0 all-gather.7.cloned.1.call-update
  36.5 0.0 all-gather.5.cloned.1.call-start
  36.6 1.1 fusion.1
  37.7 1.7 fusion.3
  39.3 0.0 all-gather.5.cloned.1.call-update
  39.4 0.0 all-gather.9.cloned.1.call-start
  39.4 1.0 fusion.44
  40.5 0.1 broadcast_in_dim.7
  40.6 0.2 all_to_all.46
  40.8 0.2 copy.24
  41.0 17.3 %all_to_all.58 = bf16[16,32,256]{2,0,1:T(8,128)(2,1)} all-to-all(bf16[16,32,256]{2,0,1:T(8,128)(2,1)S(1)} %copy.24), channel_id=1, replica_groups=mesh['section'=16,'tensor'=32] {'tensor'}, dimensions={1} | all-to-all | bytes 524288 | tf_op jit(solution)/shard_map/all_to_all | solution.py:91
  58.2 0.0 all-gather.9.cloned.1.call-update
  58.3 0.0 all-gather.11.cloned.1.call-start
  58.3 0.0 copy-done
  58.3 0.0 copy-done.1
  58.3 0.0 copy-done.3
  58.4 0.0 copy-done.2
  58.4 0.2 copy_bitcast_fusion
  58.6 16.7 %all_to_all.59 = bf16[16,32,128]{2,0,1:T(8,128)(2,1)} all-to-all(bf16[16,32,128]{2,0,1:T(8,128)(2,1)S(1)} %copy_bitcast_fusion), channel_id=1, replica_groups=mesh['section'=16,'tensor'=32] {'tensor'}, dimensions={1} | all-to-all | bytes 262144 | tf_op jit(solution)/shard_map/all_to_all | solution.py:92
  75.3 0.0 all-gather.11.cloned.1.call-update
  75.3 0.0 reduce-scatter.2.cloned.1.call-start
  76.0 0.3 multiply_sine_fusion
  76.3 0.0 all-gather.7.cloned.1.call-done
  76.4 100.0 %all-gather.5.cloned.1.call-done = bf16[256,8192]{1,0:T(8,128)(2,1)} async-done(((bf16[8,8192]{1,0:T(8,128)(2,1)}), bf16[256,8192]{1,0:T(8,128)(2,1)}) %all-gather.5.cloned.1.call-update) | async-done | bytes 4194320 | tf_op jit(solution)/shard_map/all_gather | solution.py:73
  176.4 4.4 fusion.47
  180.7 35.5 %all-gather.9.cloned.1.call-done = bf16[8192,256]{1,0:T(8,128)(2,1)} async-done(((bf16[512,256]{1,0:T(8,128)(2,1)}), bf16[8192,256]{1,0:T(8,128)(2,1)}) %all-gather.9.cloned.1.call-update) | async-done | bytes 4194320 | tf_op jit(solution)/shard_map/all_gather | solution.py:98
  216.2 5.2 %fusion.48 = f32[256,256]{0,1:T(8,128)S(1)} fusion(bf16[256,8192]{1,0:T(8,128)(2,1)} %all-gather.5.cloned.1.call-done, bf16[8192,256]{1,0:T(8,128)(2,1)} %all-gather.9.cloned.1.call-done), kind=kOutput, calls=%fused_computation.71 | convolution fusion | flops 1073741824 | bytes 8650752 | tf_op jit(solution)/shard_map/dot_general | solution.py:101
  221.4 0.3 fusion.46
  221.7 0.1 fusion.21
  221.8 35.8 %all-gather.11.cloned.1.call-done = bf16[8192,128]{1,0:T(8,128)(2,1)} async-done(((bf16[512,128]{1,0:T(8,128)(2,1)}), bf16[8192,128]{1,0:T(8,128)(2,1)}) %all-gather.11.cloned.1.call-update) | async-done | bytes 2097168 | tf_op jit(solution)/shard_map/all_gather | solution.py:104
  257.5 5.0 convolution_convert_fusion
  262.5 0.0 reduce-scatter.2.cloned.1.call-update
  262.5 234.8 %reduce-scatter.2.cloned.1.call-done = bf16[8,8192]{1,0:T(8,128)(2,1)} async-done(((bf16[256,8192]{1,0:T(8,128)(2,1)}), bf16[8,8192]{1,0:T(8,128)(2,1)}) %reduce-scatter.2.cloned.1.call-update) | async-done | bytes 131088 | tf_op jit(solution)/shard_map/reduce_scatter | solution.py:129
  (8 shorter events, 0.1 us)
Async XLA Ops:
  6.5 51.8 %copy-start = (f32[16,4096]{1,0:T(8,128)S(1)}, f32[16,4096]{1,0:T(8,128)}, u32[]{:S(2)}) copy-start(f32[16,4096]{1,0:T(8,128)} %param.26) | copy-start | bytes 786436
  6.5 51.8 %copy-start.1 = (f32[16,4096]{1,0:T(8,128)S(1)}, f32[16,4096]{1,0:T(8,128)}, u32[]{:S(2)}) copy-start(f32[16,4096]{1,0:T(8,128)} %param.27) | copy-start | bytes 786436
  6.5 51.8 %copy-start.3 = (f32[16,4096]{1,0:T(8,128)S(1)}, f32[16,4096]{1,0:T(8,128)}, u32[]{:S(2)}) copy-start(f32[16,4096]{1,0:T(8,128)} %param.28) | copy-start | bytes 786436
  6.5 51.8 %copy-start.2 = (f32[16,4096]{1,0:T(8,128)S(1)}, f32[16,4096]{1,0:T(8,128)}, u32[]{:S(2)}) copy-start(f32[16,4096]{1,0:T(8,128)} %param.29) | copy-start | bytes 786436
  6.5 69.8 %all-gather.7.cloned.1.call-start = ((), (), s32[]{:S(2)}) async-start(), calls=%async_computation.5 | async-start | bytes 2228224 | tf_op jit(solution)/shard_map/all_gather | solution.py:97
  36.5 139.8 %all-gather.5.cloned.1.call-start = ((), (), s32[]{:S(2)}) async-start(), calls=%async_computation.4 | async-start | bytes 4325376 | tf_op jit(solution)/shard_map/all_gather | solution.py:73
  39.4 176.8 %all-gather.9.cloned.1.call-start = ((), (), s32[]{:S(2)}) async-start(), calls=%async_computation.6 | async-start | bytes 4456448 | tf_op jit(solution)/shard_map/all_gather | solution.py:98
  58.3 199.3 %all-gather.11.cloned.1.call-start = ((), (), s32[]{:S(2)}) async-start(), calls=%async_computation.7 | async-start | bytes 2228224 | tf_op jit(solution)/shard_map/all_gather | solution.py:104
  75.3 422.0 %reduce-scatter.2.cloned.1.call-start = ((), (), s32[]{:S(2)}) async-start(), calls=%async_computation.8 | async-start | bytes 4325376 | tf_op jit(solution)/shard_map/reduce_scatter | solution.py:129
Sparse Core Ops, SparseCore 0:
  36.7 33.0 all-gather.6
  72.9 103.3 all-gather.4
  178.5 37.6 all-gather.8
  218.2 39.2 all-gather.10
  262.6 234.6 reduce-scatter.1
where the time goes:
time: 504 us
  waiting for transfers between devices  406 us (81%)
  blocking collectives  62.4 us (12%)
  matrix products  14.8 us (3%)
  between operations  13.9 us (3%)
  other arithmetic  5.83 us (1%)
    reduce_scatter x1, waiting for transfers between devices, on_device(): lax.psum_scatter(lax.dot_general(head_out, out_buffer, (((1,), (1,)), (()...  235 us
    all_gather x1, waiting for transfers between devices, on_device(): normed = lax.all_gather(local_rows, 'tensor', axis=0, tiled=True)  100 us
    all_gather x1, waiting for transfers between devices, on_device(): lax.all_gather(output_slice, 'section', axis=0, tiled=True)  35.8 us
    all_gather x1, waiting for transfers between devices, on_device(): keyval_rows = lax.all_gather(keyval_slice, 'section', axis=0, tiled=True)  35.5 us
    all_to_all x1, blocking collectives, on_device(): lax.all_to_all(query_weight, 'tensor', split_axis=1, concat_axis=0, tiled...  28.5 us
    all_to_all x1, blocking collectives, on_device(): lax.all_to_all(spread_heads, 'tensor', split_axis=1, concat_axis=0, tiled...  17.3 us
    all_to_all x1, blocking collectives, on_device(): lax.all_to_all(output_weight, 'tensor', split_axis=1, concat_axis=0, tile...  16.7 us
  transfers between devices with their start and end apart: 5, of which 4 were waited for; matrix products, arithmetic and copies ran while one was open for 3% of the time, Pallas kernels for 0%

commit v1 on v0

--- a/solution.py
+++ b/solution.py
@@ -95,7 +95,10 @@
     offset = jnp.int32(0)
     query_total = initial[0]
     query_rows = lax.all_gather(query_slice, "section", axis=0, tiled=True)
-    keyval_rows = lax.all_gather(keyval_slice, "section", axis=0, tiled=True)
+    keyval_rows = jnp.concatenate(
+        lax.all_to_all(jnp.stack([keyval_slice] * lax.axis_size("section")), "section", 0, 0),
+        axis=0,
+    )
     columns = lax.dynamic_slice_in_dim(normed, offset, query_rows.shape[0], 1)
     query_total = query_total + jnp.dot(columns, query_rows, preferred_element_type=jnp.float32)
     keyval_total = jnp.dot(columns, keyval_rows, preferred_element_type=jnp.float32)

time: 504 us -> 461 us (0.915)
  waiting for transfers between devices: 406 us -> 365 us
  blocking collectives: 62.4 us -> 44.9 us
  starting transfers between devices: 0.2 us -> 11.7 us
    all_gather x1 -> x0, waiting for transfers between devices: 35.5 us -> none  [on_device(): keyval_rows = lax.all_gather(keyval_slice, 'section', axis=0, tiled=True)]
    all_to_all x1 -> x0, blocking collectives: 16.7 us -> none  [on_device(): lax.all_to_all(output_weight, 'tensor', split_axis=1, concat_axis=0, tile...]
    all_to_all x0 -> x2, starting transfers between devices: none -> 11.6 us  [the longest x1 7.73 us: on_device(): lax.all_to_all(jnp.stack([keyval_slice] * lax.axis_size('section')), 'sec...]
    all_to_all x0 -> x2, waiting for transfers between devices: none -> 11.2 us  [the longest x1 11.1 us: on_device(): lax.all_to_all(output_weight, 'tensor', split_axis=1, concat_axis=0, tile...]
    all_gather x1, waiting for transfers between devices: 35.8 us -> 26.9 us  [on_device(): lax.all_gather(output_slice, 'section', axis=0, tiled=True)]
    all_gather x1, waiting for transfers between devices: 100 us -> 91.6 us  [on_device(): normed = lax.all_gather(local_rows, 'tensor', axis=0, tiled=True)]
  transfers between devices with their start and end apart: 5 -> 6, of which waited for: 4 -> 4; matrix products, arithmetic and copies ran while one was open for 3% -> 4% of each run, Pallas kernels for 0% -> 0%
where the time goes in v1:
time: 461 us
  waiting for transfers between devices  365 us (79%)
  blocking collectives  44.9 us (10%)
  matrix products  14.8 us (3%)
  between operations  13.9 us (3%)
  starting transfers between devices  11.7 us (3%)
  other arithmetic  7.59 us (2%)
    reduce_scatter x1, waiting for transfers between devices, on_device(): lax.psum_scatter(lax.dot_general(head_out, out_buffer, (((1,), (1,)), (()...  235 us
    all_gather x1, waiting for transfers between devices, on_device(): normed = lax.all_gather(local_rows, 'tensor', axis=0, tiled=True)  91.6 us
    all_to_all x1, blocking collectives, on_device(): lax.all_to_all(query_weight, 'tensor', split_axis=1, concat_axis=0, tiled...  28.5 us
    all_gather x1, waiting for transfers between devices, on_device(): lax.all_gather(output_slice, 'section', axis=0, tiled=True)  26.9 us
    all_to_all x1, blocking collectives, on_device(): lax.all_to_all(spread_heads, 'tensor', split_axis=1, concat_axis=0, tiled...  16.4 us
    all_to_all x1, waiting for transfers between devices, on_device(): lax.all_to_all(output_weight, 'tensor', split_axis=1, concat_axis=0, tile...  11.1 us
  transfers between devices with their start and end apart: 6, of which 4 were waited for; matrix products, arithmetic and copies ran while one was open for 4% of the time, Pallas kernels for 0%

profile of v1, /device:TPU:2, one launch (start us, length us, event | category | flops | bytes accessed | tf_op | source)
XLA Modules:
  0.0 460.8 jit_solution(16768873458172769386)
XLA Ops:
  6.5 0.0 all-gather.6.cloned.1.call-start
  6.5 1.4 copy_bitcast_fusion.1
  7.9 28.5 %all_to_all.59 = bf16[16,32,128]{2,0,1:T(8,128)(2,1)} all-to-all(bf16[16,32,128]{2,0,1:T(8,128)(2,1)S(1)} %copy_bitcast_fusion.1), channel_id=1, replica_groups=mesh['section'=16,'tensor'=32] {'tensor'}, dimensions={1} | all-to-all | bytes 262144 | tf_op jit(solution)/shard_map/all_to_all | solution.py:90
  36.4 0.0 all-gather.6.cloned.1.call-update
  36.4 0.0 all-gather.4.cloned.1.call-start
  36.5 1.1 fusion.1
  37.6 1.7 fusion.3
  39.2 0.0 all-gather.4.cloned.1.call-update
  39.2 2.0 copy_bitcast_fusion
  41.3 3.9 all-to-all-start.3
  45.1 1.0 fusion.44
  46.2 0.1 broadcast_in_dim.7
  46.4 0.2 all_to_all.47
  46.5 0.2 copy.24
  46.7 11.1 %all-to-all-done.3 = bf16[16,32,128]{2,0,1:T(8,128)(2,1)S(1)} async-done(((bf16[16,32,128]{2,0,1:T(8,128)(2,1)}), bf16[16,32,128]{2,0,1:T(8,128)(2,1)S(1)}, u32[]{:S(2)}, u32[]{:S(2)}) %all-to-all-start.3) | async-done | bytes 131104 | tf_op jit(solution)/shard_map/all_to_all | solution.py:92
  57.8 0.0 copy-start
  57.8 16.4 %all_to_all.60 = bf16[16,32,256]{2,0,1:T(8,128)(2,1)S(1)} all-to-all(bf16[16,32,256]{2,0,1:T(8,128)(2,1)S(1)} %copy.24), channel_id=1, replica_groups=mesh['section'=16,'tensor'=32] {'tensor'}, dimensions={1} | all-to-all | bytes 524288 | tf_op jit(solution)/shard_map/all_to_all | solution.py:91
  74.3 2.4 stack.5
  76.6 0.0 copy-done
  76.6 7.7 %all-to-all-start.2 = ((bf16[16,512,256]{2,1,0:T(8,128)(2,1)}), bf16[16,512,256]{2,1,0:T(8,128)(2,1)}, u32[]{:S(2)}, u32[]{:S(2)}) async-start(bf16[16,512,256]{2,1,0:T(8,128)(2,1)} %stack.5), calls=%async_computation.2 | async-start | bytes 8388608 | tf_op jit(solution)/shard_map/all_to_all | solution.py:99
  84.4 0.0 all-gather.8.cloned.1.call-start
  84.4 0.7 all-gather.8.cloned.1.call-update
  85.1 0.0 reduce-scatter.2.cloned.1.call-start
  85.8 0.3 multiply_sine_fusion
  86.1 0.0 all-gather.6.cloned.1.call-done
  86.2 91.6 %all-gather.4.cloned.1.call-done = bf16[256,8192]{1,0:T(8,128)(2,1)} async-done(((bf16[8,8192]{1,0:T(8,128)(2,1)}), bf16[256,8192]{1,0:T(8,128)(2,1)}) %all-gather.4.cloned.1.call-update) | async-done | bytes 4194320 | tf_op jit(solution)/shard_map/all_gather | solution.py:73
  177.8 4.4 fusion.47
  182.2 0.0 all-to-all-done.2
  182.2 5.2 %fusion.48 = f32[256,256]{0,1:T(8,128)S(1)} fusion(bf16[256,8192]{1,0:T(8,128)(2,1)} %all-gather.4.cloned.1.call-done, bf16[8192,256]{1,0:T(8,128)(2,1)} %bitcast.12), kind=kOutput, calls=%fused_computation.71 | convolution fusion | flops 1073741824 | bytes 8650752 | tf_op jit(solution)/shard_map/dot_general | solution.py:104
  187.4 0.3 fusion.46
  187.7 0.1 fusion.21
  187.8 26.9 %all-gather.8.cloned.1.call-done = bf16[8192,128]{1,0:T(8,128)(2,1)} async-done(((bf16[512,128]{1,0:T(8,128)(2,1)}), bf16[8192,128]{1,0:T(8,128)(2,1)}) %all-gather.8.cloned.1.call-update) | async-done | bytes 2097168 | tf_op jit(solution)/shard_map/all_gather | solution.py:107
  214.6 4.9 %convolution_convert_fusion = bf16[256,8192]{1,0:T(8,128)(2,1)} fusion(bf16[8192,128]{1,0:T(8,128)(2,1)} %all-gather.8.cloned.1.call-done, f32[256,256]{0,1:T(8,128)S(1)} %get-tuple-element.12, f32[256]{0:T(256)S(1)} %fusion.21, f32[256]{0:T(256)S(1)} %get-tuple-element.11, f32[256,256]{0,1:T(8,128)S(1)} %fusion.48), kind=kOutput, calls=%fused_computation | convolution fusion | flops 555974656 | bytes 6621184 | tf_op jit(solution)/shard_map/dot_general | solution.py:133
  219.6 0.0 reduce-scatter.2.cloned.1.call-update
  219.6 234.7 %reduce-scatter.2.cloned.1.call-done = bf16[8,8192]{1,0:T(8,128)(2,1)} async-done(((bf16[256,8192]{1,0:T(8,128)(2,1)}), bf16[8,8192]{1,0:T(8,128)(2,1)}) %reduce-scatter.2.cloned.1.call-update) | async-done | bytes 131088 | tf_op jit(solution)/shard_map/reduce_scatter | solution.py:132
  (8 shorter events, 0.1 us)
Async XLA Ops:
  6.5 79.6 %all-gather.6.cloned.1.call-start = ((), (), s32[]{:S(2)}) async-start(), calls=%async_computation.6 | async-start | bytes 2228224 | tf_op jit(solution)/shard_map/all_gather | solution.py:97
  36.4 141.4 %all-gather.4.cloned.1.call-start = ((), (), s32[]{:S(2)}) async-start(), calls=%async_computation.5 | async-start | bytes 4325376 | tf_op jit(solution)/shard_map/all_gather | solution.py:73
  41.3 16.6 %all-to-all-start.3 = ((bf16[16,32,128]{2,0,1:T(8,128)(2,1)}), bf16[16,32,128]{2,0,1:T(8,128)(2,1)S(1)}, u32[]{:S(2)}, u32[]{:S(2)}) async-start(bf16[16,32,128]{2,0,1:T(8,128)(2,1)} %copy_bitcast_fusion), calls=%async_computation.3 | async-start | bytes 262144 | tf_op jit(solution)/shard_map/all_to_all | solution.py:92
  57.8 18.8 %copy-start = (bf16[16,32,128]{2,0,1:T(8,128)(2,1)}, bf16[16,32,128]{2,0,1:T(8,128)(2,1)S(1)}, u32[]{:S(2)}) copy-start(bf16[16,32,128]{2,0,1:T(8,128)(2,1)S(1)} %all-to-all-done.3) | copy-start | bytes 393220
  76.6 105.6 %all-to-all-start.2 = ((bf16[16,512,256]{2,1,0:T(8,128)(2,1)}), bf16[16,512,256]{2,1,0:T(8,128)(2,1)}, u32[]{:S(2)}, u32[]{:S(2)}) async-start(bf16[16,512,256]{2,1,0:T(8,128)(2,1)} %stack.5), calls=%async_computation.2 | async-start | bytes 8388608 | tf_op jit(solution)/shard_map/all_to_all | solution.py:99
  84.4 130.3 %all-gather.8.cloned.1.call-start = ((), (), s32[]{:S(2)}) async-start(), calls=%async_computation.7 | async-start | bytes 2228224 | tf_op jit(solution)/shard_map/all_gather | solution.py:107
  85.1 369.1 %reduce-scatter.2.cloned.1.call-start = ((), (), s32[]{:S(2)}) async-start(), calls=%async_computation.8 | async-start | bytes 4325376 | tf_op jit(solution)/shard_map/reduce_scatter | solution.py:132
Sparse Core Ops, SparseCore 0:
  36.5 32.4 all-gather.5
  72.2 105.5 all-gather.3
  179.9 34.6 all-gather.7
  219.7 234.4 reduce-scatter.1
